TPU v7x, 32 devices: a whole 2x2x4 slice. The times are simulated.
32 devices in a mesh: energy: 16 (over z, y, x), space: 2 (over core).
Axes of the slice: x: 2, y: 2, z: 4, core: 2. Of those that a mesh axis runs over, the one named last changes fastest.
Arguments:
- green0: bfloat16 [128, 2, 2, 192, 192], P('energy', 'space'), may hold values from -1.5 to 1
- coupling: bfloat16 [2, 192, 192], P('space'), may hold values from -0.375 to 0.375
- pattern: int32 [2, 4, 4], P('space'), may hold values 0 or 1
- broaden: bfloat16 [128, 2, 192, 192], P('energy', 'space'), may hold values from -0.5 to 1.5
- screened: float32 [128, 2, 192, 384], P(None, 'space', 'energy'), may hold values from -6 to 6
- order: int32 [192], replicated, may hold values from 0 to 191, each once
Outputs:
- sigma: float32 [128, 2, 192, 384], P('energy', 'space')
All inputs are finite; a program needn't handle non-finite values. No bound on the sum of `pattern` on one device may be relied on, other than what follows from the above.
Results may differ from a plain program's by a relative error of at most 0.0059.
Values may be sent and summed in bfloat16 or wider, within the bound.
A program may use at most 128 MiB of HBM per device.

v0:
```python
import math

import jax
import jax.numpy as jnp
from jax import lax
from jax.sharding import PartitionSpec as P


def prefix(array, axis, combine, identity, reverse):
    count, here = (lax.axis_size(axis), lax.axis_index(axis))
    everything = jax.tree.map(lambda part: lax.all_gather(part, axis), array)
    start = jax.tree.map(
        lambda part, zero: jnp.broadcast_to(jnp.asarray(zero, part.dtype), part.shape),
        array,
        identity,
    )

    def lap(k, before):
        at = count - 1 - k if reverse else k
        reached = at > here if reverse else at < here
        new = combine(before, jax.tree.map(lambda part: part[at], everything))
        return jax.tree.map(lambda a, b: jnp.where(reached, a, b), new, before)

    return lax.fori_loop(0, count, lap, start)


def flip_last(values):
    return jnp.swapaxes(values, -1, -2)


def complex_product(left_op, right_op):

    def matmul(first_op, second):
        return jnp.einsum("eij,ejk->eik", first_op, second, preferred_element_type=jnp.float32)

    real_part = matmul(left_op[:, 0], right_op[:, 0]) - matmul(left_op[:, 1], right_op[:, 1])
    imag_part = matmul(left_op[:, 0], right_op[:, 1]) + matmul(left_op[:, 1], right_op[:, 0])
    return jnp.stack([real_part, imag_part], axis=1)


def compose(earlier, later):
    first_map, first_add = earlier
    second_map, second_add = later
    joined_map = complex_product(second_map, first_map).astype(jnp.bfloat16)
    moved = complex_product(second_map, first_add).astype(jnp.bfloat16)
    joined_add = complex_product(moved, flip_last(second_map)) + second_add.astype(jnp.float32)
    return (joined_map, joined_add.astype(jnp.bfloat16))


def lesser_rows(full_green, gamma_cell):
    weighted = jnp.einsum(
        "ecij,ejk->ecik", full_green, gamma_cell, preferred_element_type=jnp.float32
    ).astype(jnp.bfloat16)

    def outer_product(first_op, second):
        return jnp.einsum("eij,ekj->eik", first_op, second, preferred_element_type=jnp.float32)

    real_part = outer_product(weighted[:, 0], full_green[:, 1]) - outer_product(
        weighted[:, 1], full_green[:, 0]
    )
    imag_part = outer_product(weighted[:, 0], full_green[:, 0]) + outer_product(
        weighted[:, 1], full_green[:, 1]
    )
    return jnp.concatenate([real_part, imag_part], axis=-1)


def convolve(values, kernel):
    points = values.shape[0]
    half_width = values.shape[-1] // 2
    energy_ticks = jnp.arange(points, dtype=jnp.int32)
    angles = (energy_ticks[:, None] * energy_ticks[None, :] % points).astype(jnp.float32) * (
        2.0 * math.pi / points
    )
    cosine = jnp.cos(angles)
    sine = jnp.sin(angles)

    def apply_table(table, operand):
        flattened = operand.reshape(points, -1)
        return jnp.dot(table, flattened, precision=lax.Precision.HIGHEST).reshape(operand.shape)

    def forward(operand):
        with_cos = apply_table(cosine, operand)
        with_sin = apply_table(sine, operand)
        real_part = with_cos[..., :half_width] + with_sin[..., half_width:]
        imag_part = with_cos[..., half_width:] - with_sin[..., :half_width]
        return (real_part, imag_part)

    value_re, value_im = forward(values)
    kernel_re, kernel_im = forward(kernel)
    product = jnp.concatenate(
        [value_re * kernel_re - value_im * kernel_im, value_re * kernel_im + value_im * kernel_re],
        axis=-1,
    )
    with_cos = apply_table(cosine, product)
    with_sin = apply_table(sine, product)
    factor_scale = 1.0 / (points * math.sqrt(points))
    back_re = with_cos[..., :half_width] - with_sin[..., half_width:]
    back_im = with_cos[..., half_width:] + with_sin[..., :half_width]
    return jnp.concatenate([-back_im * factor_scale, back_re * factor_scale], axis=-1)


def on_device(green0, coupling, pattern, broaden, screened, order):
    green_cell = green0[:, 0]
    gamma_cell = broaden[:, 0]
    block_size = green_cell.shape[-1]
    tile_size = block_size // pattern.shape[-1]
    spread = jnp.repeat(jnp.repeat(pattern[0], tile_size, axis=0), tile_size, axis=1)
    couple = coupling[0] * spread.astype(jnp.bfloat16)
    factor = jnp.einsum(
        "ecij,jk->ecik", green_cell, couple, preferred_element_type=jnp.float32
    ).astype(jnp.bfloat16)
    factor_t = flip_last(factor)
    added_term = jnp.einsum(
        "ecij,jk->ecik", factor_t, couple, preferred_element_type=jnp.float32
    ).astype(jnp.bfloat16)
    is_first = lax.axis_index("space") == 0
    green_f = green_cell.astype(jnp.float32)
    image_cell = green_f + complex_product(
        complex_product(factor, green_cell).astype(jnp.bfloat16), factor_t
    )
    map_left = jnp.where(is_first, jnp.zeros_like(factor), factor)
    add_left = jnp.where(is_first, image_cell.astype(jnp.bfloat16), green_cell)
    diagonal_ones = jnp.eye(block_size, dtype=jnp.bfloat16)
    unit_map = jnp.broadcast_to(
        jnp.stack([diagonal_ones, jnp.zeros_like(diagonal_ones)]), factor.shape
    )
    identity_pair = (unit_map, jnp.zeros_like(factor))
    unused, carried = prefix((map_left, add_left), "space", compose, identity_pair, False)
    left_part = green_f + complex_product(
        complex_product(factor, carried).astype(jnp.bfloat16), factor_t
    )
    left_part = jnp.where(is_first, image_cell, left_part)
    unused, passed = prefix((factor_t, added_term), "space", compose, identity_pair, True)
    right_part = green_f + complex_product(
        complex_product(green_cell, passed).astype(jnp.bfloat16), green_cell
    )
    full_green = (left_part + right_part - green_f).astype(jnp.bfloat16)
    row_block = lesser_rows(full_green, gamma_cell)
    slotted = jnp.take(row_block, order, axis=1)
    gathered = lax.all_to_all(slotted, "energy", split_axis=1, concat_axis=0, tiled=True)
    sigma_slot = convolve(gathered, screened[:, 0])
    returned = lax.all_to_all(sigma_slot, "energy", split_axis=0, concat_axis=1, tiled=True)
    sigma_rows = jnp.zeros_like(returned).at[:, order, :].set(returned)
    return sigma_rows[:, None]


def solution(mesh):
    return jax.shard_map(
        on_device,
        mesh=mesh,
        in_specs=(
            P("energy", "space", None, None, None),
            P("space", None, None),
            P("space", None, None),
            P("energy", "space", None, None),
            P(None, "space", "energy", None),
            P(),
        ),
        out_specs=P("energy", "space", None, None),
        check_vma=False,
    )
```

profile of v0, /device:TPU:0, one launch (start us, length us, event | category | flops | bytes accessed | tf_op | source)
XLA Modules:
  0.0 319.2 jit_solution(9556955043317671974)
XLA Ops:
  8.6 3.7 %broadcast_select_fusion.2 = (bf16[8,2,192,192]{2,3,1,0:T(8,128)(2,1)}, bf16[192,8,2,192]{3,0,2,1:T(8,128)(2,1)}) fusion(pred[]{:T(512)S(6)} %eq.5, bf16[8,1,2,192,192]{4,3,2,1,0:T(8,128)(2,1)} %param.10, bf16[1,192,192]{1,2,0:T(8,128)(2,1)S(1)} %bitcast_multiply_fusion.1), kind=kOutput, calls=%fused_computation.91 | convolution fusion | flops 227672064 | bytes 3612673 | tf_op jit(solution)/shard_map/ecij,jk->ecik/dot_general | solution.py:109
  15.5 2.7 copy.147
  18.2 2.9 fusion.41
  22.8 2.8 copy.165
  42.2 30.2 %while.31 = (s32[]{:T(128)}, bf16[8,2,192,192]{3,2,0,1:T(8,128)(2,1)}, s32[]{:T(128)}, bf16[2,8,2,192,192]{4,3,2,1,0:T(8,128)(2,1)}, bf16[2,8,2,192,192]{4,3,2,1...) while((s32[]{:T(128)}, bf16[8,2,192,192]{3,2,0,1:T(8,128)(2,1)}, s32[]{:T(128)}, ...), condition=%wide.region_3.4_spmd.clone, body=%wide.region_2.3_spmd.clone.sunk | while | flops 911867904 | bytes 42467480 | solution.py:24
  42.2 3.4 %constant_dynamic-slice_fusion.7 = (bf16[1,8,2,192,192]{4,3,2,1,0:T(8,128)(2,1)}, bf16[1,8,2,192,192]{4,3,2,1,0:T(8,128)(2,1)S(1)}) fusion(bf16[2,8,2,192,192]{4,3,2,1,0:T(8,128)(2,1)} %get-tuple-element.448, s32[]{:T(128)S(6)} %select_n.175, bf16[2,8,2,192,192]{4,3,2,1,0:T(8,128)(2,1)} %get-tuple-element.447), kind=kLoop, calls=%fused_computation.46.clone.1 | loop fusion | bytes 4718596 | tf_op jit(solution)/shard_map/while/body/eval_jaxpr/dynamic_slice | solution.py:21
  51.2 5.0 %fusion.159 = bf16[8,2,192,192]{3,2,0,1:T(8,128)(2,1)} fusion(f32[8,1,192,192]{3,2,0,1:T(8,128)} %add_bitcast_fusion.7, f32[8,1,192,192]{3,2,0,1:T(8,128)} %subtract_bitcast_fusion.7, bf16[1,8,2,192,192]{4,3,2,1,0:T(8,128)(2,1)} %get-tuple-element.406, pred[]{:T(512)S(6)} %gt.12, bf16[8,2,192,192]{3,2,0,1:T(8,128)(2,1)} %get-tuple-element.437, ...), kind=kLoop, calls=%fused_computation.27.clone.1 | loop fusion | flops 3538944 | bytes 5898242 | tf_op jit(solution)/shard_map/while/body/eval_jaxpr/jit(_where)/select_n | solution.py:22
  56.2 3.4 %constant_dynamic-slice_fusion.7 = (bf16[1,8,2,192,192]{4,3,2,1,0:T(8,128)(2,1)}, bf16[1,8,2,192,192]{4,3,2,1,0:T(8,128)(2,1)S(1)}) fusion(bf16[2,8,2,192,192]{4,3,2,1,0:T(8,128)(2,1)} %get-tuple-element.448, s32[]{:T(128)S(6)} %select_n.175, bf16[2,8,2,192,192]{4,3,2,1,0:T(8,128)(2,1)} %get-tuple-element.447), kind=kLoop, calls=%fused_computation.46.clone.1 | loop fusion | bytes 4718596 | tf_op jit(solution)/shard_map/while/body/eval_jaxpr/dynamic_slice | solution.py:21
  66.7 5.7 %fusion.159 = bf16[8,2,192,192]{3,2,0,1:T(8,128)(2,1)} fusion(f32[8,1,192,192]{3,2,0,1:T(8,128)} %add_bitcast_fusion.7, f32[8,1,192,192]{3,2,0,1:T(8,128)} %subtract_bitcast_fusion.7, bf16[1,8,2,192,192]{4,3,2,1,0:T(8,128)(2,1)} %get-tuple-element.406, pred[]{:T(512)S(6)} %gt.12, bf16[8,2,192,192]{3,2,0,1:T(8,128)(2,1)} %get-tuple-element.437, ...), kind=kLoop, calls=%fused_computation.27.clone.1 | loop fusion | flops 3538944 | bytes 5898242 | tf_op jit(solution)/shard_map/while/body/eval_jaxpr/jit(_where)/select_n | solution.py:22
  72.4 2.9 copy.181
  82.0 28.7 %while.30 = (s32[]{:T(128)}, bf16[8,2,192,192]{3,2,0,1:T(8,128)(2,1)}, s32[]{:T(128)}, bf16[2,8,2,192,192]{4,3,2,1,0:T(8,128)(2,1)}, bf16[2,8,2,192,192]{4,3,2,1,0:T(8,128)(2,1)}, /*index=5*/s32[]{:T(128)}, s32[]{:T(128)}) while((s32[]{:T(128)}, bf16[8,2,192,192]{3,2,0,1:T(8,128)(2,1)}, s32[]{:T(128)}, ...), condition=%wide.region_1.2_spmd.clone, body=%wide.region_0.1_spmd.clone.sunk | while | flops 911867904 | bytes 42467424 | solution.py:24
  82.0 3.4 %constant_dynamic-slice_fusion.6 = (bf16[1,8,2,192,192]{4,3,2,1,0:T(8,128)(2,1)}, bf16[1,8,2,192,192]{4,3,2,1,0:T(8,128)(2,1)S(1)}) fusion(bf16[2,8,2,192,192]{4,3,2,1,0:T(8,128)(2,1)} %get-tuple-element.425, s32[]{:T(128)} %get-tuple-element.414, bf16[2,8,2,192,192]{4,3,2,1,0:T(8,128)(2,1)} %get-tuple-element.424), kind=kLoop, calls=%fused_computation.23.clone.1 | loop fusion | bytes 4718596 | tf_op jit(solution)/shard_map/while/body/eval_jaxpr/dynamic_slice | solution.py:21
  91.1 4.2 %fusion.150 = bf16[8,2,192,192]{3,2,0,1:T(8,128)(2,1)} fusion(f32[8,1,192,192]{3,2,0,1:T(8,128)} %add_bitcast_fusion.6, f32[8,1,192,192]{3,2,0,1:T(8,128)} %subtract_bitcast_fusion.6, bf16[1,8,2,192,192]{4,3,2,1,0:T(8,128)(2,1)} %get-tuple-element.399, pred[]{:T(512)S(6)} %lt.107, bf16[8,2,192,192]{3,2,0,1:T(8,128)(2,1)} %get-tuple-element.415, ...), kind=kLoop, calls=%fused_computation.4.clone.1 | loop fusion | flops 3538944 | bytes 5898242 | tf_op jit(solution)/shard_map/while/body/eval_jaxpr/jit(_where)/select_n | solution.py:22
  95.3 3.4 %constant_dynamic-slice_fusion.6 = (bf16[1,8,2,192,192]{4,3,2,1,0:T(8,128)(2,1)}, bf16[1,8,2,192,192]{4,3,2,1,0:T(8,128)(2,1)S(1)}) fusion(bf16[2,8,2,192,192]{4,3,2,1,0:T(8,128)(2,1)} %get-tuple-element.425, s32[]{:T(128)} %get-tuple-element.414, bf16[2,8,2,192,192]{4,3,2,1,0:T(8,128)(2,1)} %get-tuple-element.424), kind=kLoop, calls=%fused_computation.23.clone.1 | loop fusion | bytes 4718596 | tf_op jit(solution)/shard_map/while/body/eval_jaxpr/dynamic_slice | solution.py:21
  105.8 4.7 %fusion.150 = bf16[8,2,192,192]{3,2,0,1:T(8,128)(2,1)} fusion(f32[8,1,192,192]{3,2,0,1:T(8,128)} %add_bitcast_fusion.6, f32[8,1,192,192]{3,2,0,1:T(8,128)} %subtract_bitcast_fusion.6, bf16[1,8,2,192,192]{4,3,2,1,0:T(8,128)(2,1)} %get-tuple-element.399, pred[]{:T(512)S(6)} %lt.107, bf16[8,2,192,192]{3,2,0,1:T(8,128)(2,1)} %get-tuple-element.415, ...), kind=kLoop, calls=%fused_computation.4.clone.1 | loop fusion | flops 3538944 | bytes 5898242 | tf_op jit(solution)/shard_map/while/body/eval_jaxpr/jit(_where)/select_n | solution.py:22
  126.4 2.8 copy.204
  129.2 2.5 gather_fusion
  133.4 7.9 %all-to-all-start = ((f32[8,192,384]{2,0,1:T(8,128)}), f32[8,192,384]{2,0,1:T(8,128)}, u32[]{:S(2)}, u32[]{:S(2)}) async-start(f32[8,192,384]{2,0,1:T(8,128)} %select_bitcast_fusion), calls=%async_computation | async-start | bytes 4718592 | tf_op jit(solution)/shard_map/all_to_all | solution.py:140
  141.4 7.8 %reduce = f32[128,12,384]{2,1,0:T(8,128)} reduce(f32[128,1,12,384]{3,1,2,0:T(1,128)S(1)} %copy-done.22, f32[]{:T(128)} %constant.105), dimensions={1}, to_apply=%param.14.reduce_sub_computation | reduce | bytes 4718596 | tf_op args[4]
  149.2 4.1 %copy.271 = f32[16,8,12,384]{3,1,2,0:T(8,128)} copy(f32[16,8,12,384]{3,2,1,0:T(8,128)} %bitcast.419) | data formatting | bytes 4718592
  153.3 2.2 copy.206
  155.5 3.8 %fusion.54 = f32[128,12,384]{2,0,1:T(8,128)} fusion(f32[12,384,128]{2,1,0:T(8,128)S(1)} %bitcast.406), kind=kOutput, calls=%fused_computation.142 | convolution fusion | flops 906199040 | bytes 4718592 | tf_op jit(solution)/shard_map/dot_general | solution.py:79
  159.2 3.7 %fusion.59 = f32[128,12,384]{2,0,1:T(8,128)} fusion(f32[12,384,128]{2,1,0:T(8,128)S(1)} %bitcast.407), kind=kOutput, calls=%fused_computation.147 | convolution fusion | flops 906199040 | bytes 4718592 | tf_op jit(solution)/shard_map/dot_general | solution.py:79
  163.0 25.9 %all-to-all-done = f32[8,192,384]{2,0,1:T(8,128)} async-done(((f32[8,192,384]{2,0,1:T(8,128)}), f32[8,192,384]{2,0,1:T(8,128)}, u32[]{:S(2)}, u32[]{:S(2)}) %all-to-all-start) | async-done | bytes 2359328 | tf_op jit(solution)/shard_map/all_to_all | solution.py:140
  190.9 2.3 fusion.56
  193.3 2.3 fusion.61
  199.2 2.2 copy.207
  201.4 2.3 fusion.17
  203.8 2.3 fusion.19
  208.9 81.6 %all_to_all.33 = f32[128,12,384]{2,1,0:T(8,128)S(1)} all-to-all(f32[128,12,384]{2,1,0:T(8,128)S(1)} %copy.208), channel_id=1, replica_groups=mesh['energy'=16,'space'=2] {'energy'}, dimensions={0} | all-to-all | bytes 4718592 | tf_op jit(solution)/shard_map/all_to_all | solution.py:142
  290.5 2.2 copy.209
  293.3 17.3 %scatter_fusion = f32[8,192,384]{2,0,1:T(8,128)S(1)} fusion(f32[8,192,384]{2,0,1:T(8,128)S(1)} %broadcast_in_dim.27, s32[192]{0:T(256)S(1)} %copy-done.24, f32[192,8,384]{2,1,0:T(8,128)} %bitcast.421), kind=kCustom, calls=%fused_computation.1 | custom fusion | bytes 7078656 | tf_op jit(solution)/shard_map/scatter | solution.py:143
  (161 shorter events, 83.8 us)
Async XLA Ops:
  6.5 117.2 %copy-start = (bf16[8,1,192,192]{3,2,1,0:T(8,128)(2,1)S(1)}, bf16[8,1,192,192]{3,2,1,0:T(8,128)(2,1)}, u32[]{:S(2)}) copy-start(bf16[8,1,192,192]{3,2,1,0:T(8,128)(2,1)} %param.13) | copy-start | bytes 1769476
  6.5 34.5 %all-gather.12.cloned.1.call-start = ((), (), s32[]{:S(2)}) async-start(), calls=%async_computation.4 | async-start | bytes 4718592 | tf_op jit(solution)/shard_map/all_gather | solution.py:11
  12.3 1.4 copy-start.2
  12.3 29.9 %all-gather.14.cloned.1.call-start = ((), (), s32[]{:S(2)}) async-start(), calls=%async_computation.5 | async-start | bytes 4718592 | tf_op jit(solution)/shard_map/all_gather | solution.py:11
  15.4 66.5 %all-gather.8.cloned.1.call-start = ((), (), s32[]{:S(2)}) async-start(), calls=%async_computation.2 | async-start | bytes 4718592 | tf_op jit(solution)/shard_map/all_gather | solution.py:11
  18.2 2.9 copy-start.4
  28.2 1.4 copy-start.5
  28.2 1.9 copy-start.21
  31.1 1.2 copy-start.8
  31.1 2.5 copy-start.20
  31.6 1.2 copy-start.10
  35.9 1.6 copy-start.16
  35.9 46.0 %all-gather.10.cloned.1.call-start = ((), (), s32[]{:S(2)}) async-start(), calls=%async_computation.3 | async-start | bytes 4718592 | tf_op jit(solution)/shard_map/all_gather | solution.py:11
  39.2 0.7 copy-start.25
  39.9 0.6 copy-start.23
  72.4 2.9 copy-start.6
  75.3 1.6 copy-start.12
  110.6 2.0 copy-start.1
  110.7 2.3 copy-start.3
  114.0 1.4 copy-start.17
  114.4 1.5 copy-start.7
  114.5 2.0 copy-start.13
  116.4 1.4 copy-start.19
  117.9 1.4 copy-start.18
  120.6 1.4 copy-start.9
  120.6 1.9 copy-start.11
  129.2 2.5 copy-start.26
  133.4 7.9 %copy-start.22 = (f32[128,1,12,384]{3,1,2,0:T(1,128)S(1)}, f32[128,1,12,384]{3,1,2,0:T(1,128)}, u32[]{:S(2)}) copy-start(f32[128,1,12,384]{3,1,2,0:T(1,128)} %param.14) | copy-start | bytes 7077892
  133.4 55.4 %all-to-all-start = ((f32[8,192,384]{2,0,1:T(8,128)}), f32[8,192,384]{2,0,1:T(8,128)}, u32[]{:S(2)}, u32[]{:S(2)}) async-start(f32[8,192,384]{2,0,1:T(8,128)} %select_bitcast_fusion), calls=%async_computation | async-start | bytes 4718592 | tf_op jit(solution)/shard_map/all_to_all | solution.py:140
  193.2 2.4 copy-start.14
  193.2 2.4 copy-start.15
  292.7 0.7 copy-start.24
Sparse Core Ops, SparseCore 0:
  12.4 14.8 all-gather.11
  28.8 13.2 all-gather.13
  43.7 13.2 all-gather.7
  58.4 13.2 all-gather.9
where the time goes:
time: 325 us; the launch traced here: 319 us
  blocking collectives  81.6 us (25%)
  local copies, waits for them, and re-layouts  78.4 us (24%)
  matrix products  68.6 us (21%)
  other arithmetic  41.3 us (13%)
  waiting for transfers between devices  27.1 us (8%)
  between operations  13.7 us (4%)
  starting transfers between devices  8.2 us (3%)
    all_to_all x1, blocking collectives, on_device(): lax.all_to_all(sigma_slot, 'energy', split_axis=0, concat_axis=1, tiled=T...  81.6 us
    dot_general x56, matrix products, matmul(): jnp.einsum('eij,ejk->eik', first_op, second, preferred_element_type=jnp.f...  44.1 us
    all_to_all x1, waiting for transfers between devices, on_device(): lax.all_to_all(slotted, 'energy', split_axis=1, concat_axis=0, tiled=True)  25.9 us
    unnamed x58, local copies, waits for them, and re-layouts  23.4 us
    select_n x4, other arithmetic, lap(): return jax.tree.map(lambda a, b: jnp.where(reached, a, b), new, before)  19.5 us
    scatter x1, local copies, waits for them, and re-layouts, on_device(): sigma_rows = jnp.zeros_like(returned).at[:, order, :].set(returned)  17.3 us
    dot_general x6, matrix products, apply_table(): jnp.dot(table, flattened, precision=lax.Precision.HIGHEST)  16.8 us
    dynamic_slice x8, local copies, waits for them, and re-layouts, lap(): new = combine(before, jax.tree.map(lambda part: part[at], everything))  13.9 us
  transfers between devices with their start and end apart: 5, of which 2 were waited for; matrix products, arithmetic and copies ran while one was open for 26% of the time, Pallas kernels for 0%

commit v1 on v0

v1 whole, which is shorter than its diff:
```python
import functools
import math

import jax
import jax.numpy as jnp
import numpy as np
from jax import lax
from jax.experimental import pallas as pl
from jax.experimental.pallas import tpu as pltpu
from jax.sharding import PartitionSpec as P

F32 = jnp.float32
BF16 = jnp.bfloat16
PLAIN = ((1,), (0,))
LAST = ((1,), (1,))
FIRST = ((0,), (0,))


def dot(a, b, dims=PLAIN):
    return lax.dot_general(a, b, (dims, ((), ())), preferred_element_type=F32)


def complex_dot(left, right_re, right_im, dims=PLAIN):
    rows = left.shape[0] // 2
    with_re = dot(left, right_re, dims)
    with_im = dot(left, right_im, dims)
    return (with_re[:rows] - with_im[rows:], with_im[:rows] + with_re[rows:])


def stack(pair):
    return jnp.concatenate(pair, axis=0)


def born_kernel(first_ref, green_ref, couple_ref, send_ref, mult_ref, base_ref):
    green = green_ref[0]
    rows = green.shape[0] // 2
    couple = couple_ref[...]
    factor = dot(green, couple).astype(BF16)

    @pl.when(first_ref[0] == 1)
    def _():
        moved = stack(complex_dot(factor, green[:rows], green[rows:])).astype(BF16)
        image = green.astype(F32) + stack(complex_dot(moved, factor[:rows], factor[rows:], LAST))
        base_ref[0] = image
        send_ref[0] = image.astype(BF16)
        mult_ref[0] = green

    @pl.when(first_ref[0] == 0)
    def _():
        base_ref[0] = green.astype(F32)
        send_ref[0, :rows] = dot(factor[:rows], couple, FIRST).astype(BF16)
        send_ref[0, rows:] = dot(factor[rows:], couple, FIRST).astype(BF16)
        mult_ref[0] = factor


def lesser_kernel(
    owners, first_ref, mult_ref, got_ref, base_ref, gamma_ref, pick_ref, mix_ref, out_ref, full_s, slots_s
):
    energy = pl.program_id(0)
    mult = mult_ref[0]
    rows = mult.shape[0] // 2
    got = got_ref[0]
    moved = stack(complex_dot(mult, got[:rows], got[rows:])).astype(BF16)

    @pl.when(first_ref[0] == 1)
    def _():
        full_s[...] = (base_ref[0] + stack(complex_dot(moved, mult[:rows], mult[rows:]))).astype(BF16)

    @pl.when(first_ref[0] == 0)
    def _():
        full_s[...] = (base_ref[0] + stack(complex_dot(moved, mult[:rows], mult[rows:], LAST))).astype(BF16)

    full = full_s[...]
    weighted = dot(full, gamma_ref[0]).astype(BF16)
    pick = pick_ref[...]
    weighted = stack((dot(pick, weighted[:rows]), dot(pick, weighted[rows:]))).astype(BF16)
    with_re = dot(weighted, full[:rows], LAST)
    with_im = dot(weighted, full[rows:], LAST)
    lesser = jnp.concatenate(
        [with_im[:rows] - with_re[rows:], with_re[:rows] + with_im[rows:]], axis=1
    ).astype(BF16)
    share = rows // owners
    for r in range(share):
        slots_s[r, pl.ds(pl.multiple_of(energy * owners, owners), owners), :] = lesser[
            r * owners : (r + 1) * owners
        ]

    @pl.when(energy == pl.num_programs(0) - 1)
    def _():
        mix = mix_ref[...]
        width = lesser.shape[1]
        for r in range(share):
            out_ref[:, r * width : (r + 1) * width] = dot(mix, slots_s[r]).astype(BF16)


def times_i(values):
    half = values.shape[1] // 2
    return jnp.concatenate([-values[:, half:], values[:, :half]], axis=1)


def transform(table, upper, lower):
    both = dot(table, jnp.concatenate([upper, lower], axis=0).astype(BF16))
    points = upper.shape[0]
    return both[:points] + both[points:]


def screened_kernel(scale, table_ref, values_ref, out_ref):
    width = values_ref.shape[2]
    for r in range(values_ref.shape[1]):
        values = values_ref[:, r, :]
        out_ref[:, r * width : (r + 1) * width] = (
            transform(table_ref[...], values, times_i(values)) * scale
        )


def convolve_kernel(table_ref, values_ref, kernel_ref, out_ref):
    values = values_ref[...].astype(F32)
    kernel = kernel_ref[...]
    half = kernel.shape[1] // 2
    table = table_ref[...]
    spectrum = transform(table, values, times_i(values))
    kernel_re = jnp.concatenate([kernel[:, :half], kernel[:, :half]], axis=1)
    kernel_im = jnp.concatenate([kernel[:, half:], kernel[:, half:]], axis=1)
    product = spectrum * kernel_re + times_i(spectrum) * kernel_im
    out_ref[...] = transform(table, times_i(product), product).astype(BF16)


def restore_kernel(owners, values_ref, unmix_ref, place_ref, out_ref, slots_s):
    energy = pl.program_id(0)
    width = out_ref.shape[2]
    share = out_ref.shape[1] // owners

    @pl.when(energy == 0)
    def _():
        unmix = unmix_ref[...]
        for r in range(share):
            slots_s[r] = dot(unmix, values_ref[:, r * width : (r + 1) * width]).astype(BF16)

    at = pl.ds(pl.multiple_of(energy * owners, owners), owners)
    ordered = jnp.concatenate([slots_s[r, at, :] for r in range(share)], axis=0)
    out_ref[0] = dot(place_ref[...], ordered)


def whole(shape):
    return pl.BlockSpec(shape, lambda e: (0,) * len(shape))


def per_energy(*shape):
    return pl.BlockSpec((1,) + shape, lambda e: (e,) + (0,) * len(shape))


def params():
    return pltpu.CompilerParams(dimension_semantics=("arbitrary",))


def cost(flops, moved):
    return pl.CostEstimate(flops=int(flops), bytes_accessed=int(moved), transcendentals=0)


def on_device(owners, green0, coupling, pattern, broaden, screened, order):
    here = green0.shape[0]
    size = green0.shape[-1]
    points = screened.shape[0]
    share = size // owners
    width = 2 * size
    flat = share * width
    green = green0.reshape(here, 2 * size, size)
    gamma = broaden.reshape(here, size, size)
    tile_size = size // pattern.shape[-1]
    spread = jnp.repeat(jnp.repeat(pattern[0], tile_size, axis=0), tile_size, axis=1)
    couple = coupling[0] * spread.astype(BF16)
    first = (lax.axis_index("space") == 0).astype(jnp.int32).reshape(1)
    by_row = order.reshape(owners, share).T.reshape(-1)
    ids = jnp.arange(size, dtype=jnp.int32)
    pick = (by_row[:, None] == ids[None, :]).astype(BF16)
    place = (by_row[None, :] == ids[:, None]).astype(BF16)

    ticks = np.arange(points)
    angles = (ticks[:, None] * ticks[None, :] % points) * (2.0 * math.pi / points)
    exact = np.concatenate([np.cos(angles), -np.sin(angles)], axis=1)
    high = exact.astype(BF16)
    low = (exact - high.astype(np.float64)).astype(BF16)
    table = jnp.asarray(np.concatenate([high, low], axis=0))
    where = np.arange(here * owners)
    source = (where % here) * owners + where // here
    mix_np = (source[:, None] == where[None, :]).astype(np.float32)
    mix = jnp.asarray(mix_np.astype(BF16))
    unmix = jnp.asarray(mix_np.T.astype(BF16))

    kernel = pl.pallas_call(
        functools.partial(screened_kernel, 1.0 / (points * math.sqrt(points))),
        out_shape=jax.ShapeDtypeStruct((points, flat), F32),
        cost_estimate=cost(8.0 * points * points * flat, 8 * points * flat),
        name="screened_spectrum",
    )(table, screened.reshape(points, share, width))

    smem = pl.BlockSpec(memory_space=pltpu.SMEM)
    cell = (2 * size, size)
    work = 2.0 * here * size**3
    send, mult, base = pl.pallas_call(
        born_kernel,
        grid=(here,),
        in_specs=[smem, per_energy(*cell), whole((size, size))],
        out_specs=[per_energy(*cell)] * 3,
        out_shape=[
            jax.ShapeDtypeStruct((here,) + cell, BF16),
            jax.ShapeDtypeStruct((here,) + cell, BF16),
            jax.ShapeDtypeStruct((here,) + cell, F32),
        ],
        compiler_params=params(),
        cost_estimate=cost(10 * work, 10 * here * 2 * size * size),
        name="born",
    )(first, green, couple)
    got = lax.ppermute(send, "space", [(0, 1), (1, 0)])
    mixed = pl.pallas_call(
        functools.partial(lesser_kernel, owners),
        grid=(here,),
        in_specs=[
            smem,
            per_energy(*cell),
            per_energy(*cell),
            per_energy(*cell),
            per_energy(size, size),
            whole((size, size)),
            whole((here * owners, here * owners)),
        ],
        out_specs=whole((here * owners, flat)),
        out_shape=jax.ShapeDtypeStruct((here * owners, flat), BF16),
        scratch_shapes=[
            pltpu.VMEM(cell, BF16),
            pltpu.VMEM((share, here * owners, width), BF16),
        ],
        compiler_params=params(),
        cost_estimate=cost(16 * work, 14 * here * 2 * size * size),
        name="lesser",
    )(first, mult, got, base, gamma, pick, mix)
    gathered = lax.all_to_all(mixed, "energy", split_axis=0, concat_axis=0, tiled=True)
    column = pl.BlockSpec((points, width), lambda r: (0, r))
    sigma = pl.pallas_call(
        convolve_kernel,
        grid=(share,),
        in_specs=[whole((2 * points, 2 * points)), column, column],
        out_specs=column,
        out_shape=jax.ShapeDtypeStruct((points, flat), BF16),
        compiler_params=params(),
        cost_estimate=cost(16.0 * points * points * flat, 8 * points * flat),
        name="convolve",
    )(table, gathered, kernel)
    returned = lax.all_to_all(sigma, "energy", split_axis=0, concat_axis=0, tiled=True)
    out = pl.pallas_call(
        functools.partial(restore_kernel, owners),
        grid=(here,),
        in_specs=[
            whole((here * owners, flat)),
            whole((here * owners, here * owners)),
            whole((size, size)),
        ],
        out_specs=per_energy(size, width),
        out_shape=jax.ShapeDtypeStruct((here, size, width), F32),
        scratch_shapes=[pltpu.VMEM((share, here * owners, width), BF16)],
        compiler_params=params(),
        cost_estimate=cost(4 * work, 6 * points * flat),
        name="restore",
    )(returned, unmix, place)
    return out[:, None]


def solution(mesh):
    return jax.shard_map(
        functools.partial(on_device, mesh.shape["energy"]),
        mesh=mesh,
        in_specs=(
            P("energy", "space", None, None, None),
            P("space", None, None),
            P("space", None, None),
            P("energy", "space", None, None),
            P(None, "space", "energy", None),
            P(),
        ),
        out_specs=P("energy", "space", None, None),
        check_vma=False,
    )
```

time: 325 us -> 122 us (0.38); the launches traced: 319 us -> 121 us
  local copies, waits for them, and re-layouts: 78.4 us -> 7.03 us
  matrix products: 68.6 us -> 0 us
  blocking collectives: 81.6 us -> 36 us
  Pallas kernels: 0 us -> 45.5 us
  other arithmetic: 41.3 us -> 2.97 us
  between operations: 13.7 us -> 0.06 us
  waiting for transfers between devices: 27.1 us -> 21 us
    dot_general x69 -> x0, matrix products: 68.6 us -> none  [the longest x56 44.1 us: matmul(): jnp.einsum('eij,ejk->eik', first_op, second, preferred_element_type=jnp.f...]
    all_to_all x1, blocking collectives: 81.6 us -> 36 us  [on_device(): lax.all_to_all(sigma, 'energy', split_axis=0, concat_axis=0, tiled=True)]
    pallas_call x0 -> x5, Pallas kernels: none -> 45.5 us  [the longest x1 12.2 us: on_device(): pl.pallas_call(functools.partial(lesser_kernel, owners), grid=(here,), in...]
    unnamed x58 -> x6, local copies, waits for them, and re-layouts: 23.4 us -> 1.04 us
    select_n x7 -> x0, other arithmetic: 21.7 us -> none  [the longest x4 19.5 us: lap(): return jax.tree.map(lambda a, b: jnp.where(reached, a, b), new, before)]
    scatter x1 -> x0, local copies, waits for them, and re-layouts: 17.3 us -> none  [on_device(): sigma_rows = jnp.zeros_like(returned).at[:, order, :].set(returned)]
    dynamic_slice x8 -> x0, local copies, waits for them, and re-layouts: 13.9 us -> none  [lap(): new = combine(before, jax.tree.map(lambda part: part[at], everything))]
    unnamed x3 -> x0, other arithmetic: 7.85 us -> none
  transfers between devices with their start and end apart: 5 -> 2, of which waited for: 2 -> 2; matrix products, arithmetic and copies ran while one was open for 26% -> 2% of each run, Pallas kernels for 0% -> 5%
where the time goes in v1:
time: 122 us; the launch traced here: 121 us
  Pallas kernels  45.5 us (37%)
  blocking collectives  36 us (30%)
  waiting for transfers between devices  21 us (17%)
  starting transfers between devices  8.56 us (7%)
  local copies, waits for them, and re-layouts  7.03 us (6%)
  other arithmetic  2.97 us (2%)
    all_to_all x1, blocking collectives, on_device(): lax.all_to_all(sigma, 'energy', split_axis=0, concat_axis=0, tiled=True)  36 us
    all_to_all x1, waiting for transfers between devices, on_device(): lax.all_to_all(mixed, 'energy', split_axis=0, concat_axis=0, tiled=True)  19.2 us
    pallas_call x1, Pallas kernels, on_device(): pl.pallas_call(functools.partial(lesser_kernel, owners), grid=(here,), in...  12.2 us
    pallas_call x1, Pallas kernels, on_device(): pl.pallas_call(convolve_kernel, grid=(share,), in_specs=[whole((2 * point...  12 us
    pallas_call x1, Pallas kernels, on_device(): pl.pallas_call(born_kernel, grid=(here,), in_specs=[smem, per_energy(*cel...  9.67 us
    all_to_all x1, starting transfers between devices, on_device(): lax.all_to_all(mixed, 'energy', split_axis=0, concat_axis=0, tiled=True)  8.49 us
    pallas_call x1, Pallas kernels, on_device(): pl.pallas_call(functools.partial(screened_kernel, 1.0 / (points * math.sq...  5.97 us
    pallas_call x1, Pallas kernels, on_device(): pl.pallas_call(functools.partial(restore_kernel, owners), grid=(here,), i...  5.66 us
  transfers between devices with their start and end apart: 2, of which 2 were waited for; matrix products, arithmetic and copies ran while one was open for 2% of the time, Pallas kernels for 5%

profile of v1, /device:TPU:0, one launch (start us, length us, event | category | flops | bytes accessed | tf_op | source)
XLA Modules:
  0.0 121.1 jit_solution(6390079594787114223)
XLA Ops:
  0.0 0.7 convert_bitcast_fusion
  0.7 0.1 copy.22
  0.8 0.1 broadcast_in_dim.11
  0.9 0.1 convert_element_type.23
  1.0 0.1 copy.23
  1.1 1.5 %bitcast_multiply_fusion.couple_ref = bf16[192,192]{1,0:T(8,128)(2,1)} fusion(bf16[192,192]{1,0:T(8,128)(2,1)S(1)} %copy.23, bf16[1,192,192]{2,1,0:T(8,128)(2,1)} %param.10), kind=kLoop, calls=%fused_computation.5 | loop fusion | flops 36864 | bytes 221184 | tf_op jit(solution)/shard_map/mul | solution.py:171
  2.6 9.7 %born.1 = (bf16[8,384,192]{2,1,0:T(8,128)(2,1)}, bf16[8,384,192]{2,1,0:T(8,128)(2,1)}, f32[8,384,192]{2,1,0:T(8,128)}) custom-call(s32[1]{0:T(128)} %bitcast.first_ref, bf16[8,384,192]{2,1,0:T(8,128)(2,1)} %bitcast.30, bf16[192,192]{1,0:T(8,128)(2,1)} %bitcast_multiply_fusion.couple_ref), custom_call_target="tpu_custom_call" | custom-call | flops 1132462080 | bytes 5898240 | tf_op jit(solution)/shard_map/born/pallas_call | solution.py:200
  12.3 0.0 copy-start.2
  12.3 1.8 %copy.24 = bf16[8,384,192]{1,2,0:T(8,128)(2,1)S(1)} copy(bf16[8,384,192]{2,1,0:T(8,128)(2,1)} %get-tuple-element.9) | data formatting | bytes 2359296 | tf_op jit(solution)/shard_map/born/pallas_call | solution.py:200
  14.1 0.1 collective-permute-start
  14.2 0.0 copy-done.2
  14.2 0.1 reshape.32
  14.3 0.1 copy.25
  14.4 0.1 eq.32
  14.5 0.7 fusion.1
  15.2 1.8 %collective-permute-done = bf16[8,384,192]{1,2,0:T(8,128)(2,1)S(1)} collective-permute-done((bf16[8,384,192]{1,2,0:T(8,128)(2,1)S(1)}, bf16[8,384,192]{1,2,0:T(8,128)(2,1)S(1)}, u32[]{:S(2)}, u32[]{:S(2)}) %collective-permute-start) | collective-permute-done | bytes 1179680 | tf_op jit(solution)/shard_map/ppermute | solution.py:214
  17.1 1.6 %copy.26.got_ref = bf16[8,384,192]{2,1,0:T(8,128)(2,1)} copy(bf16[8,384,192]{1,2,0:T(8,128)(2,1)S(1)} %collective-permute-done) | data formatting | bytes 2359296 | tf_op jit(solution)/shard_map/ppermute | solution.py:214
  18.6 12.2 %lesser.1 = bf16[128,4608]{1,0:T(8,128)(2,1)} custom-call(s32[1]{0:T(128)} %bitcast.first_ref, bf16[8,384,192]{2,1,0:T(8,128)(2,1)} %get-tuple-element.8.mult_ref, bf16[8,384,192]{2,1,0:T(8,128)(2,1)} %copy.26.got_ref, f32[8,384,192]{2,1,0:T(8,128)} %get-tuple-element.10.base_ref, bf16[8,192,192]{2,1,0:T(8,128)(2,1)} %bitcast.27, ...), custom_call_target="tpu_custom_call" | custom-call | flops 1811939328 | bytes 8257536 | tf_op jit(solution)/shard_map/lesser/pallas_call | solution.py:215
  30.8 0.0 copy-start.1
  30.8 8.5 %all-to-all-start = ((bf16[16,8,4608]{2,1,0:T(8,128)(2,1)}), bf16[16,8,4608]{2,1,0:T(8,128)(2,1)S(1)}, u32[]{:S(2)}, u32[]{:S(2)}) async-start(bf16[16,8,4608]{2,1,0:T(8,128)(2,1)} %bitcast.24), calls=%async_computation | async-start | bytes 2359296 | tf_op jit(solution)/shard_map/all_to_all | solution.py:237
  39.3 0.0 copy-done.1
  39.3 1.9 %copy.32 = f32[128,1,12,384]{3,2,0,1:T(8,128)} copy(f32[128,1,12,384]{3,1,2,0:T(1,128)S(1)} %copy-done.1) | data formatting | bytes 4718592 | tf_op jit(solution)/shard_map/reshape | solution.py:195
  41.3 6.0 %screened_spectrum.1.kernel_ref = f32[128,4608]{1,0:T(8,128)} custom-call(bf16[256,256]{1,0:T(8,128)(2,1)} %constant.12.clone.table_ref, f32[128,12,384]{2,1,0:T(8,128)} %bitcast.22), custom_call_target="tpu_custom_call" | custom-call | flops 603979776 | bytes 4718592 | tf_op jit(solution)/shard_map/screened_spectrum/pallas_call | solution.py:190
  47.3 19.2 %all-to-all-done = bf16[16,8,4608]{2,1,0:T(8,128)(2,1)S(1)} async-done(((bf16[16,8,4608]{2,1,0:T(8,128)(2,1)}), bf16[16,8,4608]{2,1,0:T(8,128)(2,1)S(1)}, u32[]{:S(2)}, u32[]{:S(2)}) %all-to-all-start) | async-done | bytes 1179680 | tf_op jit(solution)/shard_map/all_to_all | solution.py:237
  66.4 0.0 copy-start
  66.4 1.0 copy-done
  67.5 12.0 %convolve.1 = bf16[128,4608]{1,0:T(8,128)(2,1)} custom-call(bf16[256,256]{1,0:T(8,128)(2,1)} %constant.12.clone.table_ref, bf16[128,4608]{1,0:T(8,128)(2,1)} %bitcast.25, f32[128,4608]{1,0:T(8,128)} %screened_spectrum.1.kernel_ref), custom_call_target="tpu_custom_call" | custom-call | flops 1207959552 | bytes 4718592 | tf_op jit(solution)/shard_map/convolve/pallas_call | solution.py:239
  79.5 36.0 %all_to_all.22 = bf16[16,8,4608]{2,1,0:T(8,128)(2,1)} all-to-all(bf16[16,8,4608]{2,1,0:T(8,128)(2,1)} %bitcast.26), channel_id=1, replica_groups=mesh['energy'=16,'space'=2] {'energy'}, dimensions={0} | all-to-all | bytes 2359296 | tf_op jit(solution)/shard_map/all_to_all | solution.py:249
  115.5 5.7 %restore.1 = f32[8,192,384]{2,1,0:T(8,128)} custom-call(bf16[128,4608]{1,0:T(8,128)(2,1)} %bitcast.23, bf16[128,128]{1,0:T(8,128)(2,1)} %constant.14.clone.unmix_ref, bf16[192,192]{1,0:T(8,128)(2,1)} %get-tuple-element.11.place_ref), custom_call_target="tpu_custom_call" | custom-call | flops 452984832 | bytes 3538944 | tf_op jit(solution)/shard_map/restore/pallas_call | solution.py:250
  (1 shorter events, 0.0 us)
Async XLA Ops:
  12.3 1.9 %copy-start.2 = (s32[192]{0:T(256)S(1)}, s32[192]{0:T(256)}, u32[]{:S(2)}) copy-start(s32[192]{0:T(256)} %param.14) | copy-start | bytes 2308
  14.1 2.9 %collective-permute-start = (bf16[8,384,192]{1,2,0:T(8,128)(2,1)S(1)}, bf16[8,384,192]{1,2,0:T(8,128)(2,1)S(1)}, u32[]{:S(2)}, u32[]{:S(2)}) collective-permute-start(bf16[8,384,192]{1,2,0:T(8,128)(2,1)S(1)} %copy.24), channel_id=1, source_target_pairs={{0,1},{1,0},{2,3},{3,2},{4,5},{5,4},{6,7},{7,6},{8,9},{9,8},{10,11... | collective-permute-start | bytes 3538952 | tf_op jit(solution)/shard_map/ppermute | solution.py:214
  30.8 8.5 %copy-start.1 = (f32[128,1,12,384]{3,1,2,0:T(1,128)S(1)}, f32[128,1,12,384]{3,1,2,0:T(1,128)}, u32[]{:S(2)}) copy-start(f32[128,1,12,384]{3,1,2,0:T(1,128)} %param.13) | copy-start | bytes 7077892
  30.8 35.6 %all-to-all-start = ((bf16[16,8,4608]{2,1,0:T(8,128)(2,1)}), bf16[16,8,4608]{2,1,0:T(8,128)(2,1)S(1)}, u32[]{:S(2)}, u32[]{:S(2)}) async-start(bf16[16,8,4608]{2,1,0:T(8,128)(2,1)} %bitcast.24), calls=%async_computation | async-start | bytes 2359296 | tf_op jit(solution)/shard_map/all_to_all | solution.py:237
  66.4 1.0 copy-start

commit v2 on v1

--- a/solution.py
+++ b/solution.py
@@ -42,14 +42,14 @@
         moved = stack(complex_dot(factor, green[:rows], green[rows:])).astype(BF16)
         image = green.astype(F32) + stack(complex_dot(moved, factor[:rows], factor[rows:], LAST))
         base_ref[0] = image
-        send_ref[0] = image.astype(BF16)
+        send_ref[0] = jnp.concatenate([image[:rows], image[rows:]], axis=1).astype(BF16)
         mult_ref[0] = green
 
     @pl.when(first_ref[0] == 0)
     def _():
         base_ref[0] = green.astype(F32)
-        send_ref[0, :rows] = dot(factor[:rows], couple, FIRST).astype(BF16)
-        send_ref[0, rows:] = dot(factor[rows:], couple, FIRST).astype(BF16)
+        added = [dot(factor[:rows], couple, FIRST), dot(factor[rows:], couple, FIRST)]
+        send_ref[0] = jnp.concatenate(added, axis=1).astype(BF16)
         mult_ref[0] = factor
 
 
@@ -60,7 +60,7 @@
     mult = mult_ref[0]
     rows = mult.shape[0] // 2
     got = got_ref[0]
-    moved = stack(complex_dot(mult, got[:rows], got[rows:])).astype(BF16)
+    moved = stack(complex_dot(mult, got[:, :rows], got[:, rows:])).astype(BF16)
 
     @pl.when(first_ref[0] == 1)
     def _():
@@ -104,25 +104,103 @@
     return both[:points] + both[points:]
 
 
-def screened_kernel(scale, table_ref, values_ref, out_ref):
-    width = values_ref.shape[2]
-    for r in range(values_ref.shape[1]):
-        values = values_ref[:, r, :]
-        out_ref[:, r * width : (r + 1) * width] = (
-            transform(table_ref[...], values, times_i(values)) * scale
+def exchange_kernel(
+    owners,
+    groups,
+    scale,
+    table_ref,
+    mixed_ref,
+    screened_ref,
+    back_ref,
+    screened_s,
+    spectrum_s,
+    got_s,
+    sigma_s,
+    away_sent,
+    away_landed,
+    back_sent,
+    back_landed,
+    own_sem,
+):
+    me = lax.axis_index("energy")
+    points, share, width = screened_s.shape
+    each = share // groups
+    span = each * width
+
+    def columns(g):
+        return pl.ds(g * span, span)
+
+    def away(g, k):
+        peer = lax.rem(me + k, owners)
+        return pltpu.make_async_remote_copy(
+            src_ref=mixed_ref.at[peer, :, columns(g)],
+            dst_ref=got_s.at[me, :, columns(g)],
+            send_sem=away_sent.at[g, k - 1],
+            recv_sem=away_landed.at[g, k - 1],
+            device_id={"energy": peer},
+            device_id_type=pl.DeviceIdType.MESH,
         )
 
-
-def convolve_kernel(table_ref, values_ref, kernel_ref, out_ref):
-    values = values_ref[...].astype(F32)
-    kernel = kernel_ref[...]
-    half = kernel.shape[1] // 2
+    def back(g, k):
+        peer = lax.rem(me + k, owners)
+        return pltpu.make_async_remote_copy(
+            src_ref=sigma_s.at[peer, :, columns(g)],
+            dst_ref=back_ref.at[me, :, columns(g)],
+            send_sem=back_sent.at[g, k - 1],
+            recv_sem=back_landed.at[g, k - 1],
+            device_id={"energy": peer},
+            device_id_type=pl.DeviceIdType.MESH,
+        )
+
+    def for_peers(action):
+        lax.fori_loop(1, owners, lambda k, c: (action(k), c)[1], 0)
+
+    barrier = pltpu.get_barrier_semaphore()
+    for_peers(
+        lambda k: pl.semaphore_signal(
+            barrier,
+            inc=1,
+            device_id={"energy": lax.rem(me + k, owners)},
+            device_id_type=pl.DeviceIdType.MESH,
+        )
+    )
+    load = pltpu.make_async_copy(screened_ref, screened_s, own_sem.at[0])
+    load.start()
+    keep = pltpu.make_async_copy(mixed_ref.at[me], got_s.at[me], own_sem.at[1])
+    keep.start()
+    pl.semaphore_wait(barrier, owners - 1)
+    for g in range(groups):
+        for_peers(lambda k: away(g, k).start())
+    load.wait()
     table = table_ref[...]
-    spectrum = transform(table, values, times_i(values))
-    kernel_re = jnp.concatenate([kernel[:, :half], kernel[:, :half]], axis=1)
-    kernel_im = jnp.concatenate([kernel[:, half:], kernel[:, half:]], axis=1)
-    product = spectrum * kernel_re + times_i(spectrum) * kernel_im
-    out_ref[...] = transform(table, times_i(product), product).astype(BF16)
+    for r in range(share):
+        values = screened_s[:, r, :]
+        spectrum_s[:, r * width : (r + 1) * width] = transform(table, values, times_i(values)) * scale
+    keep.wait()
+    half = width // 2
+    owns = []
+    for g in range(groups):
+        for_peers(lambda k: away(g, k).wait_recv())
+        for r in range(g * each, (g + 1) * each):
+            at = slice(r * width, (r + 1) * width)
+            values = got_s[:, :, at].astype(F32).reshape(points, width)
+            kernel = spectrum_s[:, at]
+            spectrum = transform(table, values, times_i(values))
+            kernel_re = jnp.concatenate([kernel[:, :half], kernel[:, :half]], axis=1)
+            kernel_im = jnp.concatenate([kernel[:, half:], kernel[:, half:]], axis=1)
+            product = spectrum * kernel_re + times_i(spectrum) * kernel_im
+            result = transform(table, times_i(product), product)
+            sigma_s[:, :, at] = result.reshape(owners, points // owners, width).astype(BF16)
+        for_peers(lambda k: back(g, k).start())
+        own = pltpu.make_async_copy(
+            sigma_s.at[me, :, columns(g)], back_ref.at[me, :, columns(g)], own_sem.at[2 + g]
+        )
+        own.start()
+        owns.append(own)
+    for g in range(groups):
+        owns[g].wait()
+        for_peers(lambda k: away(g, k).wait_send())
+        for_peers(lambda k: back(g, k).wait())
 
 
 def restore_kernel(owners, values_ref, unmix_ref, place_ref, out_ref, slots_s):
@@ -187,13 +265,6 @@
     mix = jnp.asarray(mix_np.astype(BF16))
     unmix = jnp.asarray(mix_np.T.astype(BF16))
 
-    kernel = pl.pallas_call(
-        functools.partial(screened_kernel, 1.0 / (points * math.sqrt(points))),
-        out_shape=jax.ShapeDtypeStruct((points, flat), F32),
-        cost_estimate=cost(8.0 * points * points * flat, 8 * points * flat),
-        name="screened_spectrum",
-    )(table, screened.reshape(points, share, width))
-
     smem = pl.BlockSpec(memory_space=pltpu.SMEM)
     cell = (2 * size, size)
     work = 2.0 * here * size**3
@@ -201,9 +272,9 @@
         born_kernel,
         grid=(here,),
         in_specs=[smem, per_energy(*cell), whole((size, size))],
-        out_specs=[per_energy(*cell)] * 3,
+        out_specs=[per_energy(size, width), per_energy(*cell), per_energy(*cell)],
         out_shape=[
-            jax.ShapeDtypeStruct((here,) + cell, BF16),
+            jax.ShapeDtypeStruct((here, size, width), BF16),
             jax.ShapeDtypeStruct((here,) + cell, BF16),
             jax.ShapeDtypeStruct((here,) + cell, F32),
         ],
@@ -218,7 +289,7 @@
         in_specs=[
             smem,
             per_energy(*cell),
-            per_energy(*cell),
+            per_energy(size, width),
             per_energy(*cell),
             per_energy(size, size),
             whole((size, size)),
@@ -234,19 +305,29 @@
         cost_estimate=cost(16 * work, 14 * here * 2 * size * size),
         name="lesser",
     )(first, mult, got, base, gamma, pick, mix)
-    gathered = lax.all_to_all(mixed, "energy", split_axis=0, concat_axis=0, tiled=True)
-    column = pl.BlockSpec((points, width), lambda r: (0, r))
-    sigma = pl.pallas_call(
-        convolve_kernel,
-        grid=(share,),
-        in_specs=[whole((2 * points, 2 * points)), column, column],
-        out_specs=column,
-        out_shape=jax.ShapeDtypeStruct((points, flat), BF16),
-        compiler_params=params(),
-        cost_estimate=cost(16.0 * points * points * flat, 8 * points * flat),
-        name="convolve",
-    )(table, gathered, kernel)
-    returned = lax.all_to_all(sigma, "energy", split_axis=0, concat_axis=0, tiled=True)
+    groups = max(parts for parts in range(1, 5) if share % parts == 0)
+    anywhere = pl.BlockSpec(memory_space=pl.ANY)
+    each_way = pltpu.SemaphoreType.DMA((groups, owners - 1))
+    returned = pl.pallas_call(
+        functools.partial(exchange_kernel, owners, groups, 1.0 / (points * math.sqrt(points))),
+        in_specs=[pl.BlockSpec(memory_space=pltpu.VMEM), anywhere, anywhere],
+        out_specs=anywhere,
+        out_shape=jax.ShapeDtypeStruct((owners, here, flat), BF16),
+        scratch_shapes=[
+            pltpu.VMEM((points, share, width), F32),
+            pltpu.VMEM((points, flat), F32),
+            pltpu.VMEM((owners, here, flat), BF16),
+            pltpu.VMEM((owners, here, flat), BF16),
+            each_way,
+            each_way,
+            each_way,
+            each_way,
+            pltpu.SemaphoreType.DMA((2 + groups,)),
+        ],
+        compiler_params=pltpu.CompilerParams(collective_id=0, has_side_effects=True),
+        name="exchange",
+    )(table, mixed.reshape(owners, here, flat), screened.reshape(points, share, width))
+    returned = returned.reshape(points, flat)
     out = pl.pallas_call(
         functools.partial(restore_kernel, owners),
         grid=(here,),

time: 122 us -> 95.9 us (0.79)
  Pallas kernels: 45.5 us -> 88.6 us
  blocking collectives: 36 us -> 0 us
  waiting for transfers between devices: 21 us -> 0.1 us
  starting transfers between devices: 8.56 us -> 0.01 us
  local copies, waits for them, and re-layouts: 7.03 us -> 3.7 us
    pallas_call x2 -> x1, Pallas kernels: 18 us -> 60.4 us  [on_device(): pl.pallas_call(functools.partial(exchange_kernel, owners, groups, 1.0 / (...]
    all_to_all x1 -> x0, blocking collectives: 36 us -> none  [on_device(): lax.all_to_all(sigma, 'energy', split_axis=0, concat_axis=0, tiled=True)]
    all_to_all x1 -> x0, waiting for transfers between devices: 19.2 us -> none  [on_device(): lax.all_to_all(mixed, 'energy', split_axis=0, concat_axis=0, tiled=True)]
    all_to_all x1 -> x0, starting transfers between devices: 8.49 us -> none  [on_device(): lax.all_to_all(mixed, 'energy', split_axis=0, concat_axis=0, tiled=True)]
    pallas_call x1 -> x0, local copies, waits for them, and re-layouts: 1.84 us -> none  [on_device(): pl.pallas_call(born_kernel, grid=(here,), in_specs=[smem, per_energy(*cel...]
    ppermute x1, waiting for transfers between devices: 1.83 us -> 0.1 us  [on_device(): got = lax.ppermute(send, 'space', [(0, 1), (1, 0)])]
    ppermute x1 -> x0, local copies, waits for them, and re-layouts: 1.57 us -> none  [on_device(): got = lax.ppermute(send, 'space', [(0, 1), (1, 0)])]
  transfers between devices with their start and end apart: 2 -> 1, of which waited for: 2 -> 1; matrix products, arithmetic and copies ran while one was open for 2% -> 3% of each run, Pallas kernels for 5% -> 0%
where the time goes in v2:
time: 95.9 us; the launch traced here: 95.3 us
  Pallas kernels  88.6 us (92%)
  local copies, waits for them, and re-layouts  3.7 us (4%)
  other arithmetic  2.95 us (3%)
    pallas_call x1, Pallas kernels, on_device(): pl.pallas_call(functools.partial(exchange_kernel, owners, groups, 1.0 / (...  60.4 us
    pallas_call x1, Pallas kernels, on_device(): pl.pallas_call(functools.partial(lesser_kernel, owners), grid=(here,), in...  12.6 us
    pallas_call x1, Pallas kernels, on_device(): pl.pallas_call(born_kernel, grid=(here,), in_specs=[smem, per_energy(*cel...  9.89 us
    pallas_call x1, Pallas kernels, on_device(): pl.pallas_call(functools.partial(restore_kernel, owners), grid=(here,), i...  5.69 us
    reshape x1, local copies, waits for them, and re-layouts, on_device(): screened.reshape(points, share, width)  1.97 us
  transfers between devices with their start and end apart: 1, of which 1 were waited for; matrix products, arithmetic and copies ran while one was open for 3% of the time, Pallas kernels for 0%

profile of v2, /device:TPU:0, one launch (start us, length us, event | category | flops | bytes accessed | tf_op | source)
XLA Modules:
  0.0 95.3 jit_solution(17499877044580474517)
XLA Ops:
  0.0 0.7 convert_bitcast_fusion
  0.7 0.1 copy.16
  0.8 0.1 broadcast_in_dim.11
  0.9 0.1 convert_element_type.23
  1.0 0.1 copy.17
  1.1 1.5 %bitcast_multiply_fusion.couple_ref = bf16[192,192]{1,0:T(8,128)(2,1)} fusion(bf16[192,192]{1,0:T(8,128)(2,1)S(1)} %copy.17, bf16[1,192,192]{2,1,0:T(8,128)(2,1)} %param.10), kind=kLoop, calls=%fused_computation.5 | loop fusion | flops 36864 | bytes 221184 | tf_op jit(solution)/shard_map/mul | solution.py:249
  2.6 0.0 copy-start.2
  2.6 0.0 copy-start
  2.6 9.9 %born.1 = (bf16[8,192,384]{2,1,0:T(8,128)(2,1)}, bf16[8,384,192]{2,1,0:T(8,128)(2,1)}, f32[8,384,192]{2,1,0:T(8,128)}) custom-call(s32[1]{0:T(128)} %bitcast.first_ref, bf16[8,384,192]{2,1,0:T(8,128)(2,1)} %bitcast.26, bf16[192,192]{1,0:T(8,128)(2,1)} %bitcast_multiply_fusion.couple_ref), custom_call_target="tpu_custom_call" | custom-call | flops 1132462080 | bytes 5898240 | tf_op jit(solution)/shard_map/born/pallas_call | solution.py:271
  12.5 0.0 collective-permute-start
  12.5 0.0 copy-done.2
  12.5 0.1 reshape.34
  12.6 0.1 copy.18
  12.7 0.1 eq.32
  12.8 0.0 copy-done
  12.8 2.0 %copy.24 = f32[128,1,12,384]{3,2,0,1:T(8,128)} copy(f32[128,1,12,384]{3,1,2,0:T(1,128)S(1)} %copy-done) | data formatting | bytes 4718592 | tf_op jit(solution)/shard_map/reshape | solution.py:329
  14.7 0.7 fusion.1
  15.5 0.1 collective-permute-done.got_ref
  15.6 0.0 copy-start.1
  15.6 1.1 %copy-done.1 = bf16[8,192,384]{2,1,0:T(8,128)(2,1)} copy-done((bf16[8,192,384]{2,1,0:T(8,128)(2,1)}, bf16[8,192,384]{2,1,0:T(8,128)(2,1)S(1)}, u32[]{:S(2)}) %copy-start.1) | copy-done | bytes 1179672
  16.7 12.6 %lesser.1 = bf16[128,4608]{1,0:T(8,128)(2,1)} custom-call(s32[1]{0:T(128)} %bitcast.first_ref, bf16[8,384,192]{2,1,0:T(8,128)(2,1)} %get-tuple-element.8.mult_ref, bf16[8,192,384]{2,1,0:T(8,128)(2,1)} %copy-done.1, f32[8,384,192]{2,1,0:T(8,128)} %get-tuple-element.10.base_ref, bf16[8,192,192]{2,1,0:T(8,128)(2,1)} %bitcast.23, ...), custom_call_target="tpu_custom_call" | custom-call | flops 1811939328 | bytes 8257536 | tf_op jit(solution)/shard_map/lesser/pallas_call | solution.py:286
  29.2 60.4 %exchange.1 = bf16[16,8,4608]{2,1,0:T(8,128)(2,1)} custom-call(bf16[256,256]{1,0:T(8,128)(2,1)} %constant.12.clone.table_ref, bf16[16,8,4608]{2,1,0:T(8,128)(2,1)} %bitcast.22, f32[128,12,384]{2,1,0:T(8,128)} %bitcast.20), custom_call_target="tpu_custom_call" | custom-call | tf_op jit(solution)/shard_map/exchange/pallas_call | solution.py:311
  89.7 5.7 %restore.1 = f32[8,192,384]{2,1,0:T(8,128)} custom-call(bf16[128,4608]{1,0:T(8,128)(2,1)} %bitcast.21, bf16[128,128]{1,0:T(8,128)(2,1)} %constant.14.clone.unmix_ref, bf16[192,192]{1,0:T(8,128)(2,1)} %get-tuple-element.11.place_ref), custom_call_target="tpu_custom_call" | custom-call | flops 452984832 | bytes 3538944 | tf_op jit(solution)/shard_map/restore/pallas_call | solution.py:331
  (1 shorter events, 0.0 us)
Async XLA Ops:
  2.6 9.9 %copy-start.2 = (s32[192]{0:T(256)S(1)}, s32[192]{0:T(256)}, u32[]{:S(2)}) copy-start(s32[192]{0:T(256)} %param.14) | copy-start | bytes 2308
  2.6 10.1 %copy-start = (f32[128,1,12,384]{3,1,2,0:T(1,128)S(1)}, f32[128,1,12,384]{3,1,2,0:T(1,128)}, u32[]{:S(2)}) copy-start(f32[128,1,12,384]{3,1,2,0:T(1,128)} %param.13) | copy-start | bytes 7077892
  12.5 3.1 %collective-permute-start = (bf16[8,192,384]{2,1,0:T(8,128)(2,1)}, bf16[8,192,384]{2,1,0:T(8,128)(2,1)S(1)}, u32[]{:S(2)}, u32[]{:S(2)}) collective-permute-start(bf16[8,192,384]{2,1,0:T(8,128)(2,1)} %get-tuple-element.9), channel_id=1, source_target_pairs={{0,1},{1,0},{2,3},{3,2},{4,5},{5,4},{6,7},{7,6},{8,9},{9,8},{10,11... | collective-permute-start | bytes 3538952 | tf_op jit(solution)/shard_map/ppermute | solution.py:285
  15.6 1.1 %copy-start.1 = (bf16[8,192,384]{2,1,0:T(8,128)(2,1)}, bf16[8,192,384]{2,1,0:T(8,128)(2,1)S(1)}, u32[]{:S(2)}) copy-start(bf16[8,192,384]{2,1,0:T(8,128)(2,1)S(1)} %collective-permute-done.got_ref) | copy-start | bytes 3538948

commit v3 on v2

--- a/solution.py
+++ b/solution.py
@@ -31,64 +31,96 @@
     return jnp.concatenate(pair, axis=0)
 
 
-def born_kernel(first_ref, green_ref, couple_ref, send_ref, mult_ref, base_ref):
-    green = green_ref[0]
-    rows = green.shape[0] // 2
-    couple = couple_ref[...]
-    factor = dot(green, couple).astype(BF16)
+def born_kernel(first_ref, pattern_ref, green_ref, coupling_ref, send_ref, mult_ref, base_ref, couple_s):
+    many, both, size = green_ref.shape
+    rows = both // 2
+    batch = range(many)
+
+    @pl.when(pl.program_id(0) == 0)
+    def _():
+        tiles = pattern_ref.shape[0]
+        tile_size = size // tiles
+        lane = lax.broadcasted_iota(jnp.int32, (tile_size, size), 1)
+        for i in range(tiles):
+            keep = jnp.zeros((tile_size, size), F32)
+            for j in range(tiles):
+                inside = (lane >= j * tile_size) & (lane < (j + 1) * tile_size)
+                keep = jnp.where(inside, pattern_ref[i, j].astype(F32), keep)
+            at = slice(i * tile_size, (i + 1) * tile_size)
+            couple_s[at, :] = (coupling_ref[at, :].astype(F32) * keep).astype(BF16)
+
+    couple = couple_s[...]
+    green = [green_ref[i] for i in batch]
+    factor = [dot(g, couple).astype(BF16) for g in green]
 
     @pl.when(first_ref[0] == 1)
     def _():
-        moved = stack(complex_dot(factor, green[:rows], green[rows:])).astype(BF16)
-        image = green.astype(F32) + stack(complex_dot(moved, factor[:rows], factor[rows:], LAST))
-        base_ref[0] = image
-        send_ref[0] = jnp.concatenate([image[:rows], image[rows:]], axis=1).astype(BF16)
-        mult_ref[0] = green
+        moved = [
+            stack(complex_dot(f, g[:rows], g[rows:])).astype(BF16) for f, g in zip(factor, green)
+        ]
+        for i in batch:
+            re, im = complex_dot(moved[i], factor[i][:rows], factor[i][rows:], LAST)
+            re = green[i][:rows].astype(F32) + re
+            im = green[i][rows:].astype(F32) + im
+            base_ref[i, :rows] = re
+            base_ref[i, rows:] = im
+            send_ref[i] = jnp.concatenate([re, im], axis=1).astype(BF16)
+            mult_ref[i] = green[i]
 
     @pl.when(first_ref[0] == 0)
     def _():
-        base_ref[0] = green.astype(F32)
-        added = [dot(factor[:rows], couple, FIRST), dot(factor[rows:], couple, FIRST)]
-        send_ref[0] = jnp.concatenate(added, axis=1).astype(BF16)
-        mult_ref[0] = factor
+        for i in batch:
+            base_ref[i] = green[i].astype(F32)
+            added = [dot(factor[i][:rows], couple, FIRST), dot(factor[i][rows:], couple, FIRST)]
+            send_ref[i] = jnp.concatenate(added, axis=1).astype(BF16)
+            mult_ref[i] = factor[i]
 
 
 def lesser_kernel(
     owners, first_ref, mult_ref, got_ref, base_ref, gamma_ref, pick_ref, mix_ref, out_ref, full_s, slots_s
 ):
-    energy = pl.program_id(0)
-    mult = mult_ref[0]
-    rows = mult.shape[0] // 2
-    got = got_ref[0]
-    moved = stack(complex_dot(mult, got[:, :rows], got[:, rows:])).astype(BF16)
+    step = pl.program_id(0)
+    many, both, size = mult_ref.shape
+    rows = both // 2
+    batch = range(many)
+    mult = [mult_ref[i] for i in batch]
+    moved = [
+        stack(complex_dot(mult[i], got_ref[i, :, :rows], got_ref[i, :, rows:])).astype(BF16)
+        for i in batch
+    ]
+
+    def finish(dims):
+        for i in batch:
+            extra = stack(complex_dot(moved[i], mult[i][:rows], mult[i][rows:], dims))
+            full_s[i] = (base_ref[i] + extra).astype(BF16)
 
     @pl.when(first_ref[0] == 1)
     def _():
-        full_s[...] = (base_ref[0] + stack(complex_dot(moved, mult[:rows], mult[rows:]))).astype(BF16)
+        finish(PLAIN)
 
     @pl.when(first_ref[0] == 0)
     def _():
-        full_s[...] = (base_ref[0] + stack(complex_dot(moved, mult[:rows], mult[rows:], LAST))).astype(BF16)
-
-    full = full_s[...]
-    weighted = dot(full, gamma_ref[0]).astype(BF16)
+        finish(LAST)
+
+    full = [full_s[i] for i in batch]
     pick = pick_ref[...]
-    weighted = stack((dot(pick, weighted[:rows]), dot(pick, weighted[rows:]))).astype(BF16)
-    with_re = dot(weighted, full[:rows], LAST)
-    with_im = dot(weighted, full[rows:], LAST)
-    lesser = jnp.concatenate(
-        [with_im[:rows] - with_re[rows:], with_re[:rows] + with_im[rows:]], axis=1
-    ).astype(BF16)
+    weighted = [dot(full[i], gamma_ref[i]).astype(BF16) for i in batch]
+    weighted = [stack((dot(pick, w[:rows]), dot(pick, w[rows:]))).astype(BF16) for w in weighted]
     share = rows // owners
-    for r in range(share):
-        slots_s[r, pl.ds(pl.multiple_of(energy * owners, owners), owners), :] = lesser[
-            r * owners : (r + 1) * owners
-        ]
-
-    @pl.when(energy == pl.num_programs(0) - 1)
+    for i in batch:
+        with_re = dot(weighted[i], full[i][:rows], LAST)
+        with_im = dot(weighted[i], full[i][rows:], LAST)
+        lesser = jnp.concatenate(
+            [with_im[:rows] - with_re[rows:], with_re[:rows] + with_im[rows:]], axis=1
+        ).astype(BF16)
+        at = pl.ds(pl.multiple_of((step * many + i) * owners, owners), owners)
+        for r in range(share):
+            slots_s[r, at, :] = lesser[r * owners : (r + 1) * owners]
+
+    @pl.when(step == pl.num_programs(0) - 1)
     def _():
         mix = mix_ref[...]
-        width = lesser.shape[1]
+        width = 2 * size
         for r in range(share):
             out_ref[:, r * width : (r + 1) * width] = dot(mix, slots_s[r]).astype(BF16)
 
@@ -204,27 +236,28 @@
 
 
 def restore_kernel(owners, values_ref, unmix_ref, place_ref, out_ref, slots_s):
-    energy = pl.program_id(0)
-    width = out_ref.shape[2]
-    share = out_ref.shape[1] // owners
-
-    @pl.when(energy == 0)
+    step = pl.program_id(0)
+    many, size, width = out_ref.shape
+    share = size // owners
+
+    @pl.when(step == 0)
     def _():
         unmix = unmix_ref[...]
         for r in range(share):
             slots_s[r] = dot(unmix, values_ref[:, r * width : (r + 1) * width]).astype(BF16)
 
-    at = pl.ds(pl.multiple_of(energy * owners, owners), owners)
-    ordered = jnp.concatenate([slots_s[r, at, :] for r in range(share)], axis=0)
-    out_ref[0] = dot(place_ref[...], ordered)
+    for i in range(many):
+        at = pl.ds(pl.multiple_of((step * many + i) * owners, owners), owners)
+        ordered = jnp.concatenate([slots_s[r, at, :] for r in range(share)], axis=0)
+        out_ref[i] = dot(place_ref[...], ordered)
 
 
 def whole(shape):
     return pl.BlockSpec(shape, lambda e: (0,) * len(shape))
 
 
-def per_energy(*shape):
-    return pl.BlockSpec((1,) + shape, lambda e: (e,) + (0,) * len(shape))
+def energies(many, *shape):
+    return pl.BlockSpec((many,) + shape, lambda e: (e,) + (0,) * len(shape))
 
 
 def params():
@@ -244,9 +277,7 @@
     flat = share * width
     green = green0.reshape(here, 2 * size, size)
     gamma = broaden.reshape(here, size, size)
-    tile_size = size // pattern.shape[-1]
-    spread = jnp.repeat(jnp.repeat(pattern[0], tile_size, axis=0), tile_size, axis=1)
-    couple = coupling[0] * spread.astype(BF16)
+    many = max(count for count in (1, 2, 4) if here % count == 0)
     first = (lax.axis_index("space") == 0).astype(jnp.int32).reshape(1)
     by_row = order.reshape(owners, share).T.reshape(-1)
     ids = jnp.arange(size, dtype=jnp.int32)
@@ -270,35 +301,36 @@
     work = 2.0 * here * size**3
     send, mult, base = pl.pallas_call(
         born_kernel,
-        grid=(here,),
-        in_specs=[smem, per_energy(*cell), whole((size, size))],
-        out_specs=[per_energy(size, width), per_energy(*cell), per_energy(*cell)],
+        grid=(here // many,),
+        in_specs=[smem, smem, energies(many, *cell), whole((size, size))],
+        out_specs=[energies(many, size, width), energies(many, *cell), energies(many, *cell)],
         out_shape=[
             jax.ShapeDtypeStruct((here, size, width), BF16),
             jax.ShapeDtypeStruct((here,) + cell, BF16),
             jax.ShapeDtypeStruct((here,) + cell, F32),
         ],
+        scratch_shapes=[pltpu.VMEM((size, size), BF16)],
         compiler_params=params(),
         cost_estimate=cost(10 * work, 10 * here * 2 * size * size),
         name="born",
-    )(first, green, couple)
+    )(first, pattern[0], green, coupling[0])
     got = lax.ppermute(send, "space", [(0, 1), (1, 0)])
     mixed = pl.pallas_call(
         functools.partial(lesser_kernel, owners),
-        grid=(here,),
+        grid=(here // many,),
         in_specs=[
             smem,
-            per_energy(*cell),
-            per_energy(size, width),
-            per_energy(*cell),
-            per_energy(size, size),
+            energies(many, *cell),
+            energies(many, size, width),
+            energies(many, *cell),
+            energies(many, size, size),
             whole((size, size)),
             whole((here * owners, here * owners)),
         ],
         out_specs=whole((here * owners, flat)),
         out_shape=jax.ShapeDtypeStruct((here * owners, flat), BF16),
         scratch_shapes=[
-            pltpu.VMEM(cell, BF16),
+            pltpu.VMEM((many,) + cell, BF16),
             pltpu.VMEM((share, here * owners, width), BF16),
         ],
         compiler_params=params(),
@@ -330,13 +362,13 @@
     returned = returned.reshape(points, flat)
     out = pl.pallas_call(
         functools.partial(restore_kernel, owners),
-        grid=(here,),
+        grid=(here // many,),
         in_specs=[
             whole((here * owners, flat)),
             whole((here * owners, here * owners)),
             whole((size, size)),
         ],
-        out_specs=per_energy(size, width),
+        out_specs=energies(many, size, width),
         out_shape=jax.ShapeDtypeStruct((here, size, width), F32),
         scratch_shapes=[pltpu.VMEM((share, here * owners, width), BF16)],
         compiler_params=params(),

time: 95.9 us -> 82.2 us (0.86)
  Pallas kernels: 88.6 us -> 77.8 us
  other arithmetic: 2.95 us -> 0.73 us
    pallas_call x3, Pallas kernels: 28.1 us -> 17.6 us  [the longest x1 8.06 us: on_device(): pl.pallas_call(functools.partial(lesser_kernel, owners), grid=(here // ma...]
    mul x1 -> x0, other arithmetic: 1.54 us -> none  [on_device(): couple = coupling[0] * spread.astype(BF16)]
  transfers between devices with their start and end apart: 1 -> 1, of which waited for: 1 -> 1; matrix products, arithmetic and copies ran while one was open for 3% -> 4% of each run, Pallas kernels for 0% -> 0%
where the time goes in v3:
time: 82.2 us; the launch traced here: 81.9 us
  Pallas kernels  77.8 us (95%)
  local copies, waits for them, and re-layouts  3.32 us (4%)
    pallas_call x1, Pallas kernels, on_device(): pl.pallas_call(functools.partial(exchange_kernel, owners, groups, 1.0 / (...  60.2 us
    pallas_call x1, Pallas kernels, on_device(): pl.pallas_call(functools.partial(lesser_kernel, owners), grid=(here // ma...  8.06 us
    pallas_call x1, Pallas kernels, on_device(): pl.pallas_call(born_kernel, grid=(here // many,), in_specs=[smem, smem, e...  5.95 us
    pallas_call x1, Pallas kernels, on_device(): pl.pallas_call(functools.partial(restore_kernel, owners), grid=(here // m...  3.56 us
    reshape x1, local copies, waits for them, and re-layouts, on_device(): screened.reshape(points, share, width)  1.97 us
  transfers between devices with their start and end apart: 1, of which 1 were waited for; matrix products, arithmetic and copies ran while one was open for 4% of the time, Pallas kernels for 0%

profile of v3, /device:TPU:0, one launch (start us, length us, event | category | flops | bytes accessed | tf_op | source)
XLA Modules:
  0.0 81.9 jit_solution(13896586459436259818)
XLA Ops:
  0.0 0.0 copy-start.2
  0.0 0.0 copy-start
  0.0 5.9 %born.1 = (bf16[8,192,384]{2,1,0:T(8,128)(2,1)}, bf16[8,384,192]{2,1,0:T(8,128)(2,1)}, f32[8,384,192]{2,1,0:T(8,128)}) custom-call(s32[1]{0:T(128)} %bitcast.first_ref, s32[4,4]{1,0:T(4,128)} %bitcast.22, bf16[8,384,192]{2,1,0:T(8,128)(2,1)} %bitcast.20, bf16[192,192]{1,0:T(8,128)(2,1)} %bitcast.21), custom_call_target="tpu_custom_call" | custom-call | flops 1132462080 | bytes 5898240 | tf_op jit(solution)/shard_map/born/pallas_call | solution.py:302
  6.0 0.0 collective-permute-start
  6.0 0.0 copy-done.2
  6.0 0.1 reshape.29
  6.0 0.1 copy.14
  6.1 0.1 eq.32
  6.2 0.0 copy-done
  6.2 2.0 %copy.20 = f32[128,1,12,384]{3,2,0,1:T(8,128)} copy(f32[128,1,12,384]{3,1,2,0:T(1,128)S(1)} %copy-done) | data formatting | bytes 4718592 | tf_op jit(solution)/shard_map/reshape | solution.py:361
  8.2 0.7 fusion.1
  8.9 0.1 collective-permute-done.got_ref
  9.0 0.0 copy-start.1
  9.0 1.1 %copy-done.1 = bf16[8,192,384]{2,1,0:T(8,128)(2,1)} copy-done((bf16[8,192,384]{2,1,0:T(8,128)(2,1)}, bf16[8,192,384]{2,1,0:T(8,128)(2,1)S(1)}, u32[]{:S(2)}) %copy-start.1) | copy-done | bytes 1179672
  10.1 8.1 %lesser.1 = bf16[128,4608]{1,0:T(8,128)(2,1)} custom-call(s32[1]{0:T(128)} %bitcast.first_ref, bf16[8,384,192]{2,1,0:T(8,128)(2,1)} %get-tuple-element.8.mult_ref, bf16[8,192,384]{2,1,0:T(8,128)(2,1)} %copy-done.1, f32[8,384,192]{2,1,0:T(8,128)} %get-tuple-element.10.base_ref, bf16[8,192,192]{2,1,0:T(8,128)(2,1)} %bitcast.18, ...), custom_call_target="tpu_custom_call" | custom-call | flops 1811939328 | bytes 8257536 | tf_op jit(solution)/shard_map/lesser/pallas_call | solution.py:318
  18.2 60.2 %exchange.1 = bf16[16,8,4608]{2,1,0:T(8,128)(2,1)} custom-call(bf16[256,256]{1,0:T(8,128)(2,1)} %constant.12.clone.table_ref, bf16[16,8,4608]{2,1,0:T(8,128)(2,1)} %bitcast.17, f32[128,12,384]{2,1,0:T(8,128)} %bitcast.15), custom_call_target="tpu_custom_call" | custom-call | tf_op jit(solution)/shard_map/exchange/pallas_call | solution.py:343
  78.4 3.6 %restore.1 = f32[8,192,384]{2,1,0:T(8,128)} custom-call(bf16[128,4608]{1,0:T(8,128)(2,1)} %bitcast.16, bf16[128,128]{1,0:T(8,128)(2,1)} %constant.14.clone.unmix_ref, bf16[192,192]{1,0:T(8,128)(2,1)} %get-tuple-element.11.place_ref), custom_call_target="tpu_custom_call" | custom-call | flops 452984832 | bytes 3538944 | tf_op jit(solution)/shard_map/restore/pallas_call | solution.py:363
Async XLA Ops:
  0.0 6.0 %copy-start.2 = (s32[192]{0:T(256)S(1)}, s32[192]{0:T(256)}, u32[]{:S(2)}) copy-start(s32[192]{0:T(256)} %param.14) | copy-start | bytes 2308
  0.0 6.2 %copy-start = (f32[128,1,12,384]{3,1,2,0:T(1,128)S(1)}, f32[128,1,12,384]{3,1,2,0:T(1,128)}, u32[]{:S(2)}) copy-start(f32[128,1,12,384]{3,1,2,0:T(1,128)} %param.13) | copy-start | bytes 7077892
  6.0 3.1 %collective-permute-start = (bf16[8,192,384]{2,1,0:T(8,128)(2,1)}, bf16[8,192,384]{2,1,0:T(8,128)(2,1)S(1)}, u32[]{:S(2)}, u32[]{:S(2)}) collective-permute-start(bf16[8,192,384]{2,1,0:T(8,128)(2,1)} %get-tuple-element.9), channel_id=1, source_target_pairs={{0,1},{1,0},{2,3},{3,2},{4,5},{5,4},{6,7},{7,6},{8,9},{9,8},{10,11... | collective-permute-start | bytes 3538952 | tf_op jit(solution)/shard_map/ppermute | solution.py:317
  9.0 1.1 %copy-start.1 = (bf16[8,192,384]{2,1,0:T(8,128)(2,1)}, bf16[8,192,384]{2,1,0:T(8,128)(2,1)S(1)}, u32[]{:S(2)}) copy-start(bf16[8,192,384]{2,1,0:T(8,128)(2,1)S(1)} %collective-permute-done.got_ref) | copy-start | bytes 3538948

commit v4 on v3

--- a/solution.py
+++ b/solution.py
@@ -337,7 +337,7 @@
         cost_estimate=cost(16 * work, 14 * here * 2 * size * size),
         name="lesser",
     )(first, mult, got, base, gamma, pick, mix)
-    groups = max(parts for parts in range(1, 5) if share % parts == 0)
+    groups = max(parts for parts in range(1, 7) if share % parts == 0)
     anywhere = pl.BlockSpec(memory_space=pl.ANY)
     each_way = pltpu.SemaphoreType.DMA((groups, owners - 1))
     returned = pl.pallas_call(

time: 82.2 us -> 83.9 us (1.021)
  Pallas kernels: 77.8 us -> 79.6 us
    pallas_call x1, Pallas kernels: 60.2 us -> 62 us  [on_device(): pl.pallas_call(functools.partial(exchange_kernel, owners, groups, 1.0 / (...]
where the time goes in v4:
time: 83.9 us; the launch traced here: 83.8 us
  Pallas kernels  79.6 us (95%)
  local copies, waits for them, and re-layouts  3.32 us (4%)
    pallas_call x1, Pallas kernels, on_device(): pl.pallas_call(functools.partial(exchange_kernel, owners, groups, 1.0 / (...  62 us
    pallas_call x1, Pallas kernels, on_device(): pl.pallas_call(functools.partial(lesser_kernel, owners), grid=(here // ma...  8.06 us
    pallas_call x1, Pallas kernels, on_device(): pl.pallas_call(born_kernel, grid=(here // many,), in_specs=[smem, smem, e...  5.95 us
    pallas_call x1, Pallas kernels, on_device(): pl.pallas_call(functools.partial(restore_kernel, owners), grid=(here // m...  3.56 us
    reshape x1, local copies, waits for them, and re-layouts, on_device(): screened.reshape(points, share, width)  1.97 us
  transfers between devices with their start and end apart: 1, of which 1 were waited for; matrix products, arithmetic and copies ran while one was open for 4% of the time, Pallas kernels for 0%

profile of v4, /device:TPU:0, one launch (start us, length us, event | category | flops | bytes accessed | tf_op | source)
XLA Modules:
  0.0 83.8 jit_solution(5499849195402151707)
XLA Ops:
  0.0 0.0 copy-start.2
  0.0 0.0 copy-start
  0.0 5.9 %born.1 = (bf16[8,192,384]{2,1,0:T(8,128)(2,1)}, bf16[8,384,192]{2,1,0:T(8,128)(2,1)}, f32[8,384,192]{2,1,0:T(8,128)}) custom-call(s32[1]{0:T(128)} %bitcast.first_ref, s32[4,4]{1,0:T(4,128)} %bitcast.22, bf16[8,384,192]{2,1,0:T(8,128)(2,1)} %bitcast.20, bf16[192,192]{1,0:T(8,128)(2,1)} %bitcast.21), custom_call_target="tpu_custom_call" | custom-call | flops 1132462080 | bytes 5898240 | tf_op jit(solution)/shard_map/born/pallas_call | solution.py:302
  6.0 0.0 collective-permute-start
  6.0 0.0 copy-done.2
  6.0 0.1 reshape.29
  6.0 0.1 copy.14
  6.1 0.1 eq.32
  6.2 0.0 copy-done
  6.2 2.0 %copy.20 = f32[128,1,12,384]{3,2,0,1:T(8,128)} copy(f32[128,1,12,384]{3,1,2,0:T(1,128)S(1)} %copy-done) | data formatting | bytes 4718592 | tf_op jit(solution)/shard_map/reshape | solution.py:361
  8.2 0.7 fusion.1
  8.9 0.1 collective-permute-done.got_ref
  9.0 0.0 copy-start.1
  9.0 1.1 %copy-done.1 = bf16[8,192,384]{2,1,0:T(8,128)(2,1)} copy-done((bf16[8,192,384]{2,1,0:T(8,128)(2,1)}, bf16[8,192,384]{2,1,0:T(8,128)(2,1)S(1)}, u32[]{:S(2)}) %copy-start.1) | copy-done | bytes 1179672
  10.1 8.1 %lesser.1 = bf16[128,4608]{1,0:T(8,128)(2,1)} custom-call(s32[1]{0:T(128)} %bitcast.first_ref, bf16[8,384,192]{2,1,0:T(8,128)(2,1)} %get-tuple-element.8.mult_ref, bf16[8,192,384]{2,1,0:T(8,128)(2,1)} %copy-done.1, f32[8,384,192]{2,1,0:T(8,128)} %get-tuple-element.10.base_ref, bf16[8,192,192]{2,1,0:T(8,128)(2,1)} %bitcast.18, ...), custom_call_target="tpu_custom_call" | custom-call | flops 1811939328 | bytes 8257536 | tf_op jit(solution)/shard_map/lesser/pallas_call | solution.py:318
  18.2 62.0 %exchange.1 = bf16[16,8,4608]{2,1,0:T(8,128)(2,1)} custom-call(bf16[256,256]{1,0:T(8,128)(2,1)} %constant.12.clone.table_ref, bf16[16,8,4608]{2,1,0:T(8,128)(2,1)} %bitcast.17, f32[128,12,384]{2,1,0:T(8,128)} %bitcast.15), custom_call_target="tpu_custom_call" | custom-call | tf_op jit(solution)/shard_map/exchange/pallas_call | solution.py:343
  80.2 3.6 %restore.1 = f32[8,192,384]{2,1,0:T(8,128)} custom-call(bf16[128,4608]{1,0:T(8,128)(2,1)} %bitcast.16, bf16[128,128]{1,0:T(8,128)(2,1)} %constant.14.clone.unmix_ref, bf16[192,192]{1,0:T(8,128)(2,1)} %get-tuple-element.11.place_ref), custom_call_target="tpu_custom_call" | custom-call | flops 452984832 | bytes 3538944 | tf_op jit(solution)/shard_map/restore/pallas_call | solution.py:363
Async XLA Ops:
  0.0 6.0 %copy-start.2 = (s32[192]{0:T(256)S(1)}, s32[192]{0:T(256)}, u32[]{:S(2)}) copy-start(s32[192]{0:T(256)} %param.14) | copy-start | bytes 2308
  0.0 6.2 %copy-start = (f32[128,1,12,384]{3,1,2,0:T(1,128)S(1)}, f32[128,1,12,384]{3,1,2,0:T(1,128)}, u32[]{:S(2)}) copy-start(f32[128,1,12,384]{3,1,2,0:T(1,128)} %param.13) | copy-start | bytes 7077892
  6.0 3.1 %collective-permute-start = (bf16[8,192,384]{2,1,0:T(8,128)(2,1)}, bf16[8,192,384]{2,1,0:T(8,128)(2,1)S(1)}, u32[]{:S(2)}, u32[]{:S(2)}) collective-permute-start(bf16[8,192,384]{2,1,0:T(8,128)(2,1)} %get-tuple-element.9), channel_id=1, source_target_pairs={{0,1},{1,0},{2,3},{3,2},{4,5},{5,4},{6,7},{7,6},{8,9},{9,8},{10,11... | collective-permute-start | bytes 3538952 | tf_op jit(solution)/shard_map/ppermute | solution.py:317
  9.0 1.1 %copy-start.1 = (bf16[8,192,384]{2,1,0:T(8,128)(2,1)}, bf16[8,192,384]{2,1,0:T(8,128)(2,1)S(1)}, u32[]{:S(2)}) copy-start(bf16[8,192,384]{2,1,0:T(8,128)(2,1)S(1)} %collective-permute-done.got_ref) | copy-start | bytes 3538948
